TPU v7x, 512 devices: a whole 4x8x8 slice. The times are simulated.
512 devices in a mesh: chan: 8 (over z), sx: 8 (over x, core), sy: 8 (over y).
Axes of the slice: x: 4, y: 8, z: 8, core: 2. Of those that a mesh axis runs over, the one named last changes fastest.
Arguments:
- volume: bfloat16 [8, 64, 64, 256], P('sx', 'sy', None, 'chan'), may hold values from -6 to 6
- kernel: bfloat16 [27, 256, 256], P(None, 'chan'), may hold values from -0.078125 to 0.078125
- grad_out: bfloat16 [8, 64, 64, 256], P('sx', 'sy', None, 'chan'), may hold values from -6 to 6
Outputs:
- out: bfloat16 [8, 64, 64, 256], P('sx', 'sy', None, 'chan')
- grad_input: bfloat16 [8, 64, 64, 256], P('sx', 'sy', None, 'chan')
- grad_kernel: float32 [27, 256, 256], P(None, 'chan')
All inputs are finite; a program needn't handle non-finite values.
Results may differ from a plain program's by a relative error of at most 0.0015.
Values may be sent and summed in bfloat16 or wider, within the bound.
No kernel may reach another device: no remote copies, remote signals or barrier semaphores. Data moves between devices by JAX's collectives and lax.ppermute only.
A program may use at most 64 MiB of HBM per device.

v0:
```python
import math
import jax
import jax.numpy as jnp
from jax import lax
from jax.sharding import PartitionSpec as P


def padded_2(shard, sides, width):
    for axis, dim in sides:
        count, length = (lax.axis_size(axis), shard.shape[dim])
        up = [(i, (i + 1) % count) for i in range(count - 1)]
        down = [(j, i) for i, j in up]
        last = lax.slice_in_dim(shard, length - width, length, axis=dim)
        leading = lax.slice_in_dim(shard, 0, width, axis=dim)
        before = lax.ppermute(last, axis, up)
        after = lax.ppermute(leading, axis, down)
        shard = jnp.concatenate([before, shard, after], axis=dim)
    return shard


def body(volume, kernel, grad_out):
    size_x, size_y, size_z, own_in = volume.shape
    total_out = kernel.shape[2]
    cells = size_x * size_y * size_z
    rim = padded_2(volume, (("sx", 0), ("sy", 1)), 1)
    padded = jnp.pad(rim, ((0, 0), (0, 0), (1, 1), (0, 0)))
    offsets = [(index // 9, index // 3 % 3, index % 3) for index in range(27)]
    partial_out = jnp.zeros((cells, total_out), jnp.float32)
    for index in range(27):
        a, b, e = offsets[index]
        window = padded[a : a + size_x, b : b + size_y, e : e + size_z].reshape(cells, own_in)
        partial_out = partial_out + jnp.dot(
            window, kernel[index], preferred_element_type=jnp.float32
        )
    partial_out = partial_out.reshape(size_x, size_y, size_z, total_out)
    out = lax.psum_scatter(partial_out, "chan", scatter_dimension=3, tiled=True).astype(
        jnp.bfloat16
    )
    grad_full = lax.all_gather(grad_out, "chan", axis=3, tiled=True)
    grad_rimmed = padded_2(grad_full, (("sx", 0), ("sy", 1)), 1)
    grad_padded = jnp.pad(grad_rimmed, ((0, 0), (0, 0), (1, 1), (0, 0)))
    flat_grad = grad_full.reshape(cells, total_out)
    back = jnp.zeros((cells, own_in), jnp.float32)
    kernel_terms = []
    for index in range(27):
        a, b, e = offsets[index]
        window = grad_padded[
            2 - a : 2 - a + size_x, 2 - b : 2 - b + size_y, 2 - e : 2 - e + size_z
        ].reshape(cells, total_out)
        back = back + lax.dot_general(
            window, kernel[index], (((1,), (1,)), ((), ())), preferred_element_type=jnp.float32
        )
        in_window = padded[a : a + size_x, b : b + size_y, e : e + size_z].reshape(cells, own_in)
        kernel_terms.append(
            lax.dot_general(
                in_window, flat_grad, (((0,), (0,)), ((), ())), preferred_element_type=jnp.float32
            )
        )
    grad_input = back.reshape(size_x, size_y, size_z, own_in).astype(jnp.bfloat16)
    local_kernel = jnp.stack(kernel_terms)
    summed = lax.psum(local_kernel, ("sx", "sy"))
    all_cells = cells * lax.axis_size("sx") * lax.axis_size("sy")
    grad_kernel = summed / jnp.float32(math.sqrt(all_cells))
    return (out, grad_input, grad_kernel)


def solution(mesh):
    return jax.shard_map(
        body,
        mesh=mesh,
        in_specs=(P("sx", "sy", None, "chan"), P(None, "chan", None), P("sx", "sy", None, "chan")),
        out_specs=(P("sx", "sy", None, "chan"), P("sx", "sy", None, "chan"), P(None, "chan", None)),
        check_vma=False,
    )
```

profile of v0, /device:TPU:25, one launch (start us, length us, event | category | flops | bytes accessed | tf_op | source)
XLA Modules:
  0.0 342.9 jit_solution(3898932481704692713)
XLA Ops:
  8.1 3.7 %collective-permute-start = (bf16[1,8,64,32]{2,3,1,0:T(8,128)(2,1)}, bf16[1,8,64,32]{2,3,1,0:T(8,128)(2,1)S(1)}, u32[]{:S(2)}, u32[]{:S(2)}) collective-permute-start(bf16[1,8,64,32]{2,3,1,0:T(8,128)(2,1)} %param.3), channel_id=1, source_target_pairs={{0,8},{8,16},{16,24},{24,32},{32,40},{40,48},{48,56},{1,9},{9,17},... | collective-permute-start | bytes 98312 | tf_op jit(solution)/shard_map/ppermute | solution.py:15
  11.7 1.9 collective-permute-start.1
  15.5 2.1 collective-permute-done.1
  17.6 2.1 collective-permute-start.3
  19.7 4.4 %collective-permute-start.2 = (bf16[3,1,64,32]{2,3,1,0:T(8,128)(2,1)S(1)}, bf16[3,1,64,32]{2,3,1,0:T(8,128)(2,1)S(1)}, u32[]{:S(2)}, u32[]{:S(2)}) collective-permute-start(bf16[3,1,64,32]{2,3,1,0:T(8,128)(2,1)S(1)} %get-tuple-element.68), channel_id=1, source_target_pairs={{0,1},{1,2},{2,3},{3,4},{4,5},{5,6},{6,7},{8,9},{9,10},{10,11},{11... | collective-permute-start | bytes 36872 | tf_op jit(solution)/shard_map/ppermute | solution.py:15
  24.1 26.2 %all_gather.3 = bf16[1,8,64,256]{2,1,0,3:T(8,128)(2,1)S(1)} all-gather(bf16[1,8,64,32]{2,1,0,3:T(8,128)(2,1)S(1)} %copy.98), channel_id=1, replica_groups=mesh['chan'=8,'sx'=8,'sy'=8] {'chan'}, dimensions={3}, use_global_device_ids=true | all-gather | bytes 294912 | tf_op jit(solution)/shard_map/all_gather | solution.py:39
  50.6 5.5 %collective-permute-start.5 = (bf16[1,8,64,256]{3,2,1,0:T(8,128)(2,1)S(1)}, bf16[1,8,64,256]{3,2,1,0:T(8,128)(2,1)S(1)}, u32[]{:S(2)}, u32[]{:S(2)}) collective-permute-start(bf16[1,8,64,256]{3,2,1,0:T(8,128)(2,1)S(1)} %copy.99), channel_id=1, source_target_pairs={{8,0},{16,8},{24,16},{32,24},{40,32},{48,40},{56,48},{9,1},{17,9},... | collective-permute-start | bytes 786440 | tf_op jit(solution)/shard_map/ppermute | solution.py:16
  56.1 4.7 %collective-permute-start.4 = (bf16[1,8,64,256]{3,2,1,0:T(8,128)(2,1)S(1)}, bf16[1,8,64,256]{3,2,1,0:T(8,128)(2,1)S(1)}, u32[]{:S(2)}, u32[]{:S(2)}) collective-permute-start(bf16[1,8,64,256]{3,2,1,0:T(8,128)(2,1)S(1)} %copy.99), channel_id=1, source_target_pairs={{0,8},{8,16},{16,24},{24,32},{32,40},{40,48},{48,56},{1,9},{9,17},... | collective-permute-start | bytes 786440 | tf_op jit(solution)/shard_map/ppermute | solution.py:15
  74.5 1.6 reshape.329
  77.6 1.6 reshape.330
  83.7 1.6 reshape.332
  88.1 1.6 reshape.334
  90.3 1.6 reshape.335
  93.4 1.6 reshape.337
  96.4 1.6 reshape.338
  100.9 1.6 reshape.340
  103.9 1.6 reshape.341
  109.2 1.6 reshape.343
  112.2 1.6 reshape.344
  114.5 1.6 reshape.347
  146.8 1.9 collective-permute-start.7
  148.7 4.8 %collective-permute-start.6 = (bf16[3,1,64,256]{3,2,1,0:T(8,128)(2,1)S(1)}, bf16[3,1,64,256]{3,2,1,0:T(8,128)(2,1)S(1)}, u32[]{:S(2)}, u32[]{:S(2)}) collective-permute-start(bf16[3,1,64,256]{3,2,1,0:T(8,128)(2,1)S(1)} %get-tuple-element.39), channel_id=1, source_target_pairs={{0,1},{1,2},{2,3},{3,4},{4,5},{5,6},{6,7},{8,9},{9,10},{10,11},{11... | collective-permute-start | bytes 294920 | tf_op jit(solution)/shard_map/ppermute | solution.py:15
  162.8 168.9 %all-reduce.4.cloned.1.call-done = f32[27,32,256]{2,1,0:T(8,128)} async-done(((f32[27,32,256]{2,1,0:T(8,128)}), f32[27,32,256]{2,1,0:T(8,128)}) %all-reduce.4.cloned.1.call-update) | async-done | bytes 884752 | tf_op jit(solution)/shard_map/psum | solution.py:61
  331.7 2.2 broadcast_multiply_fusion
  (229 shorter events, 79.6 us)
Async XLA Ops:
  8.0 52.8 %copy-start.4 = (bf16[1,8,64,32]{2,3,1,0:T(8,128)(2,1)S(1)}, bf16[1,8,64,32]{2,3,1,0:T(8,128)(2,1)}, u32[]{:S(2)}) copy-start(bf16[1,8,64,32]{2,3,1,0:T(8,128)(2,1)} %param.3) | copy-start | bytes 98308
  8.0 323.7 %all-reduce.4.cloned.1.call-start = ((), (), s32[]{:S(2)}) async-start(), calls=%async_computation.2 | async-start | bytes 1769472 | tf_op jit(solution)/shard_map/psum | solution.py:61
  8.1 6.5 %collective-permute-start = (bf16[1,8,64,32]{2,3,1,0:T(8,128)(2,1)}, bf16[1,8,64,32]{2,3,1,0:T(8,128)(2,1)S(1)}, u32[]{:S(2)}, u32[]{:S(2)}) collective-permute-start(bf16[1,8,64,32]{2,3,1,0:T(8,128)(2,1)} %param.3), channel_id=1, source_target_pairs={{0,8},{8,16},{16,24},{24,32},{32,40},{40,48},{48,56},{1,9},{9,17},... | collective-permute-start | bytes 98312 | tf_op jit(solution)/shard_map/ppermute | solution.py:15
  11.7 5.8 %collective-permute-start.1 = (bf16[1,8,64,32]{2,3,1,0:T(8,128)(2,1)}, bf16[1,8,64,32]{2,3,1,0:T(8,128)(2,1)S(1)}, u32[]{:S(2)}, u32[]{:S(2)}) collective-permute-start(bf16[1,8,64,32]{2,3,1,0:T(8,128)(2,1)} %param.3), channel_id=1, source_target_pairs={{8,0},{16,8},{24,16},{32,24},{40,32},{48,40},{56,48},{9,1},{17,9},... | collective-permute-start | bytes 98312 | tf_op jit(solution)/shard_map/ppermute | solution.py:16
  14.6 47.1 %copy-start.8 = (bf16[1,8,64,32]{2,3,1,0:T(8,128)(2,1)}, bf16[1,8,64,32]{2,3,1,0:T(8,128)(2,1)S(1)}, u32[]{:S(2)}) copy-start(bf16[1,8,64,32]{2,3,1,0:T(8,128)(2,1)S(1)} %collective-permute-done) | copy-start | bytes 98308
  17.5 45.0 %copy-start.6 = (bf16[1,8,64,32]{2,3,1,0:T(8,128)(2,1)}, bf16[1,8,64,32]{2,3,1,0:T(8,128)(2,1)S(1)}, u32[]{:S(2)}) copy-start(bf16[1,8,64,32]{2,3,1,0:T(8,128)(2,1)S(1)} %collective-permute-done.1) | copy-start | bytes 98308
  17.6 44.9 %collective-permute-start.3 = (bf16[3,1,64,32]{2,3,1,0:T(8,128)(2,1)S(1)}, bf16[3,1,64,32]{2,3,1,0:T(8,128)(2,1)S(1)}, u32[]{:S(2)}, u32[]{:S(2)}) collective-permute-start(bf16[3,1,64,32]{2,3,1,0:T(8,128)(2,1)S(1)} %get-tuple-element.69), channel_id=1, source_target_pairs={{1,0},{2,1},{3,2},{4,3},{5,4},{6,5},{7,6},{9,8},{10,9},{11,10},{12... | collective-permute-start | bytes 36872 | tf_op jit(solution)/shard_map/ppermute | solution.py:16
  19.7 42.9 %collective-permute-start.2 = (bf16[3,1,64,32]{2,3,1,0:T(8,128)(2,1)S(1)}, bf16[3,1,64,32]{2,3,1,0:T(8,128)(2,1)S(1)}, u32[]{:S(2)}, u32[]{:S(2)}) collective-permute-start(bf16[3,1,64,32]{2,3,1,0:T(8,128)(2,1)S(1)} %get-tuple-element.68), channel_id=1, source_target_pairs={{0,1},{1,2},{2,3},{3,4},{4,5},{5,6},{6,7},{8,9},{9,10},{10,11},{11... | collective-permute-start | bytes 36872 | tf_op jit(solution)/shard_map/ppermute | solution.py:15
  50.6 96.1 %collective-permute-start.5 = (bf16[1,8,64,256]{3,2,1,0:T(8,128)(2,1)S(1)}, bf16[1,8,64,256]{3,2,1,0:T(8,128)(2,1)S(1)}, u32[]{:S(2)}, u32[]{:S(2)}) collective-permute-start(bf16[1,8,64,256]{3,2,1,0:T(8,128)(2,1)S(1)} %copy.99), channel_id=1, source_target_pairs={{8,0},{16,8},{24,16},{32,24},{40,32},{48,40},{56,48},{9,1},{17,9},... | collective-permute-start | bytes 786440 | tf_op jit(solution)/shard_map/ppermute | solution.py:16
  56.1 90.7 %collective-permute-start.4 = (bf16[1,8,64,256]{3,2,1,0:T(8,128)(2,1)S(1)}, bf16[1,8,64,256]{3,2,1,0:T(8,128)(2,1)S(1)}, u32[]{:S(2)}, u32[]{:S(2)}) collective-permute-start(bf16[1,8,64,256]{3,2,1,0:T(8,128)(2,1)S(1)} %copy.99), channel_id=1, source_target_pairs={{0,8},{8,16},{16,24},{24,32},{32,40},{40,48},{48,56},{1,9},{9,17},... | collective-permute-start | bytes 786440 | tf_op jit(solution)/shard_map/ppermute | solution.py:15
  63.9 2.3 copy-start
  68.5 18.9 %copy-start.14 = (bf16[1,8,64,32]{2,3,1,0:T(8,128)(2,1)S(1)}, bf16[1,8,64,32]{2,3,1,0:T(8,128)(2,1)}, u32[]{:S(2)}) copy-start(bf16[1,8,64,32]{2,3,1,0:T(8,128)(2,1)} %get-tuple-element.51) | copy-start | bytes 98308
  68.5 21.2 %copy-start.13 = (bf16[1,8,64,32]{2,3,1,0:T(8,128)(2,1)S(1)}, bf16[1,8,64,32]{2,3,1,0:T(8,128)(2,1)}, u32[]{:S(2)}) copy-start(bf16[1,8,64,32]{2,3,1,0:T(8,128)(2,1)} %get-tuple-element.50) | copy-start | bytes 98308
  74.5 25.7 %copy-start.12 = (bf16[1,8,64,32]{2,3,1,0:T(8,128)(2,1)S(1)}, bf16[1,8,64,32]{2,3,1,0:T(8,128)(2,1)}, u32[]{:S(2)}) copy-start(bf16[1,8,64,32]{2,3,1,0:T(8,128)(2,1)} %get-tuple-element.47) | copy-start | bytes 98308
  88.1 25.7 %copy-start.11 = (bf16[1,8,64,32]{2,3,1,0:T(8,128)(2,1)S(1)}, bf16[1,8,64,32]{2,3,1,0:T(8,128)(2,1)}, u32[]{:S(2)}) copy-start(bf16[1,8,64,32]{2,3,1,0:T(8,128)(2,1)} %get-tuple-element.42) | copy-start | bytes 98308
  90.3 25.7 %copy-start.3 = (bf16[1,8,64,32]{2,3,1,0:T(8,128)(2,1)S(1)}, bf16[1,8,64,32]{2,3,1,0:T(8,128)(2,1)}, u32[]{:S(2)}) copy-start(bf16[1,8,64,32]{2,3,1,0:T(8,128)(2,1)} %copy-done.2) | copy-start | bytes 98308
  102.4 16.1 %copy-start.9 = (bf16[1,8,64,32]{2,3,1,0:T(8,128)(2,1)S(1)}, bf16[1,8,64,32]{2,3,1,0:T(8,128)(2,1)}, u32[]{:S(2)}) copy-start(bf16[1,8,64,32]{2,3,1,0:T(8,128)(2,1)} %copy-done.8) | copy-start | bytes 98308
  116.0 5.0 %copy-start.1 = (bf16[1,8,64,32]{2,3,1,0:T(8,128)(2,1)S(1)}, bf16[1,8,64,32]{2,3,1,0:T(8,128)(2,1)}, u32[]{:S(2)}) copy-start(bf16[1,8,64,32]{2,3,1,0:T(8,128)(2,1)} %get-tuple-element.60) | copy-start | bytes 98308
  121.0 5.0 %copy-start.5 = (bf16[1,8,64,32]{2,3,1,0:T(8,128)(2,1)S(1)}, bf16[1,8,64,32]{2,3,1,0:T(8,128)(2,1)}, u32[]{:S(2)}) copy-start(bf16[1,8,64,32]{2,3,1,0:T(8,128)(2,1)} %param.3) | copy-start | bytes 98308
  128.6 5.0 %copy-start.7 = (bf16[1,8,64,32]{2,3,1,0:T(8,128)(2,1)S(1)}, bf16[1,8,64,32]{2,3,1,0:T(8,128)(2,1)}, u32[]{:S(2)}) copy-start(bf16[1,8,64,32]{2,3,1,0:T(8,128)(2,1)} %copy-done.6) | copy-start | bytes 98308
  134.4 3.5 %copy-start.17 = (bf16[512,32]{0,1:T(8,128)(2,1)S(1)}, bf16[512,32]{0,1:T(8,128)(2,1)}, u32[]{:S(2)}) copy-start(bf16[512,32]{0,1:T(8,128)(2,1)} %reshape.324) | copy-start | bytes 98308
  137.8 196.1 %reduce-scatter.2.cloned.1.call-start = ((), (), s32[]{:S(2)}) async-start(), calls=%async_computation.1 | async-start | bytes 1179648 | tf_op jit(solution)/shard_map/reduce_scatter | solution.py:36
  146.8 8.3 %collective-permute-start.7 = (bf16[3,1,64,256]{3,2,1,0:T(8,128)(2,1)S(1)}, bf16[3,1,64,256]{3,2,1,0:T(8,128)(2,1)S(1)}, u32[]{:S(2)}, u32[]{:S(2)}) collective-permute-start(bf16[3,1,64,256]{3,2,1,0:T(8,128)(2,1)S(1)} %get-tuple-element.40), channel_id=1, source_target_pairs={{1,0},{2,1},{3,2},{4,3},{5,4},{6,5},{7,6},{9,8},{10,9},{11,10},{12... | collective-permute-start | bytes 294920 | tf_op jit(solution)/shard_map/ppermute | solution.py:16
  148.7 6.4 %collective-permute-start.6 = (bf16[3,1,64,256]{3,2,1,0:T(8,128)(2,1)S(1)}, bf16[3,1,64,256]{3,2,1,0:T(8,128)(2,1)S(1)}, u32[]{:S(2)}, u32[]{:S(2)}) collective-permute-start(bf16[3,1,64,256]{3,2,1,0:T(8,128)(2,1)S(1)} %get-tuple-element.39), channel_id=1, source_target_pairs={{0,1},{1,2},{2,3},{3,4},{4,5},{5,6},{6,7},{8,9},{9,10},{10,11},{11... | collective-permute-start | bytes 294920 | tf_op jit(solution)/shard_map/ppermute | solution.py:15
  (24 other events, 18.4 us)
Sparse Core Ops, SparseCore 0:
  137.9 193.7 all-reduce.3
Sparse Core Ops, SparseCore 1:
  155.2 32.7 reduce-scatter.1
where the time goes:
time: 345 us; the launch traced here: 343 us
  waiting for transfers between devices  171 us (50%)
  local copies, waits for them, and re-layouts  60 us (17%)
  matrix products  34.2 us (10%)
  starting transfers between devices  29 us (8%)
  blocking collectives  26.2 us (8%)
  between operations  16.2 us (5%)
  other arithmetic  6.23 us (2%)
    psum x1, waiting for transfers between devices, body(): summed = lax.psum(local_kernel, ('sx', 'sy'))  169 us
    reshape x27, local copies, waits for them, and re-layouts, body(): padded[a:a + size_x, b:b + size_y, e:e + size_z].reshape(cells, own_in)  29.3 us
    all_gather x1, blocking collectives, body(): grad_full = lax.all_gather(grad_out, 'chan', axis=3, tiled=True)  26.2 us
    dot_general x27, matrix products, body(): lax.dot_general(in_window, flat_grad, (((0,), (0,)), ((), ())), preferred...  22.6 us
    slice x25, local copies, waits for them, and re-layouts, body(): padded[a:a + size_x, b:b + size_y, e:e + size_z].reshape(cells, own_in)  21 us
    ppermute x4, starting transfers between devices, padded_2(): before = lax.ppermute(last, axis, up)  17.6 us
    ppermute x4, starting transfers between devices, padded_2(): after = lax.ppermute(leading, axis, down)  11.4 us
    unnamed x81, local copies, waits for them, and re-layouts  6.98 us
  transfers between devices with their start and end apart: 10, of which 2 were waited for; matrix products, arithmetic and copies ran while one was open for 28% of the time, Pallas kernels for 0%

commit v1 on v0

--- a/solution.py
+++ b/solution.py
@@ -58,7 +58,9 @@
         )
     grad_input = back.reshape(size_x, size_y, size_z, own_in).astype(jnp.bfloat16)
     local_kernel = jnp.stack(kernel_terms)
-    summed = lax.psum(local_kernel, ("sx", "sy"))
+    summed = local_kernel
+    for over in ("sy", "sx"):
+        summed = lax.psum(summed, over)
     all_cells = cells * lax.axis_size("sx") * lax.axis_size("sy")
     grad_kernel = summed / jnp.float32(math.sqrt(all_cells))
     return (out, grad_input, grad_kernel)

time: 345 us -> 299 us (0.87)
  the two profiles are of different devices: /device:TPU:25 before, /device:TPU:8 now
where the time goes in v1:
time: 299 us; the launch traced here: 297 us
  waiting for transfers between devices  131 us (44%)
  local copies, waits for them, and re-layouts  58.5 us (20%)
  matrix products  34.2 us (11%)
  blocking collectives  29.5 us (10%)
  starting transfers between devices  21.4 us (7%)
  between operations  16.2 us (5%)
  other arithmetic  6.23 us (2%)
    psum x2, waiting for transfers between devices, body(): summed = lax.psum(summed, over)  128 us
    all_gather x1, blocking collectives, body(): grad_full = lax.all_gather(grad_out, 'chan', axis=3, tiled=True)  29.5 us
    reshape x27, local copies, waits for them, and re-layouts, body(): padded[a:a + size_x, b:b + size_y, e:e + size_z].reshape(cells, own_in)  28.7 us
    dot_general x27, matrix products, body(): lax.dot_general(in_window, flat_grad, (((0,), (0,)), ((), ())), preferred...  22.6 us
    slice x25, local copies, waits for them, and re-layouts, body(): padded[a:a + size_x, b:b + size_y, e:e + size_z].reshape(cells, own_in)  20.1 us
    ppermute x4, starting transfers between devices, padded_2(): after = lax.ppermute(leading, axis, down)  10.9 us
    ppermute x4, starting transfers between devices, padded_2(): before = lax.ppermute(last, axis, up)  10.2 us
    unnamed x81, local copies, waits for them, and re-layouts  6.88 us
  transfers between devices with their start and end apart: 11, of which 4 were waited for; matrix products, arithmetic and copies ran while one was open for 31% of the time, Pallas kernels for 0%

profile of v1, /device:TPU:8, one launch (start us, length us, event | category | flops | bytes accessed | tf_op | source)
XLA Modules:
  0.0 296.7 jit_solution(2149509360669573494)
XLA Ops:
  8.1 1.7 collective-permute-start
  12.9 1.6 collective-permute-done.1
  14.5 6.0 %collective-permute-start.3 = (bf16[3,1,64,32]{2,3,1,0:T(8,128)(2,1)S(1)}, bf16[3,1,64,32]{2,3,1,0:T(8,128)(2,1)S(1)}, u32[]{:S(2)}, u32[]{:S(2)}) collective-permute-start(bf16[3,1,64,32]{2,3,1,0:T(8,128)(2,1)S(1)} %get-tuple-element.69), channel_id=1, source_target_pairs={{1,0},{2,1},{3,2},{4,3},{5,4},{6,5},{7,6},{9,8},{10,9},{11,10},{12... | collective-permute-start | bytes 36872 | tf_op jit(solution)/shard_map/ppermute | solution.py:16
  20.5 1.9 collective-permute-start.2
  22.4 29.5 %all_gather.3 = bf16[1,8,64,256]{2,1,0,3:T(8,128)(2,1)S(1)} all-gather(bf16[1,8,64,32]{2,1,0,3:T(8,128)(2,1)S(1)} %copy.98), channel_id=1, replica_groups=mesh['chan'=8,'sx'=8,'sy'=8] {'chan'}, dimensions={3}, use_global_device_ids=true | all-gather | bytes 294912 | tf_op jit(solution)/shard_map/all_gather | solution.py:39
  53.6 3.0 %collective-permute-start.4 = (bf16[1,8,64,256]{3,2,1,0:T(8,128)(2,1)S(1)}, bf16[1,8,64,256]{3,2,1,0:T(8,128)(2,1)S(1)}, u32[]{:S(2)}, u32[]{:S(2)}) collective-permute-start(bf16[1,8,64,256]{3,2,1,0:T(8,128)(2,1)S(1)} %copy.99), channel_id=1, source_target_pairs={{0,8},{8,16},{16,24},{24,32},{32,40},{40,48},{48,56},{1,9},{9,17},... | collective-permute-start | bytes 786440 | tf_op jit(solution)/shard_map/ppermute | solution.py:15
  67.2 1.6 reshape.325
  70.3 1.6 reshape.326
  73.3 1.6 reshape.329
  76.3 1.6 reshape.330
  81.6 1.6 reshape.332
  83.8 1.6 reshape.333
  86.0 1.6 reshape.334
  89.1 1.6 reshape.335
  92.1 1.6 reshape.337
  94.3 1.6 reshape.338
  101.2 1.6 reshape.341
  106.5 1.6 reshape.343
  108.7 1.6 reshape.344
  141.2 2.3 collective-permute-start.7
  143.5 3.5 %collective-permute-start.6 = (bf16[3,1,64,256]{3,2,1,0:T(8,128)(2,1)S(1)}, bf16[3,1,64,256]{3,2,1,0:T(8,128)(2,1)S(1)}, u32[]{:S(2)}, u32[]{:S(2)}) collective-permute-start(bf16[3,1,64,256]{3,2,1,0:T(8,128)(2,1)S(1)} %get-tuple-element.39), channel_id=1, source_target_pairs={{0,1},{1,2},{2,3},{3,4},{4,5},{5,6},{6,7},{8,9},{9,10},{10,11},{11... | collective-permute-start | bytes 294920 | tf_op jit(solution)/shard_map/ppermute | solution.py:15
  156.5 56.5 %all-reduce.5.cloned.1.call-done = f32[27,32,256]{2,1,0:T(8,128)} async-done(((f32[27,32,256]{2,1,0:T(8,128)}), f32[27,32,256]{2,1,0:T(8,128)}) %all-reduce.5.cloned.1.call-update) | async-done | bytes 884752 | tf_op jit(solution)/shard_map/psum | solution.py:63
  215.7 71.4 %all-reduce.7.cloned.1.call-done = f32[27,32,256]{2,1,0:T(8,128)} async-done(((f32[27,32,256]{2,1,0:T(8,128)}), f32[27,32,256]{2,1,0:T(8,128)}) %all-reduce.7.cloned.1.call-update) | async-done | bytes 884752 | tf_op jit(solution)/shard_map/psum | solution.py:63
  287.1 2.2 broadcast_multiply_fusion
  (232 shorter events, 80.4 us)
Async XLA Ops:
  8.0 48.6 %copy-start.4 = (bf16[1,8,64,32]{2,3,1,0:T(8,128)(2,1)S(1)}, bf16[1,8,64,32]{2,3,1,0:T(8,128)(2,1)}, u32[]{:S(2)}) copy-start(bf16[1,8,64,32]{2,3,1,0:T(8,128)(2,1)} %param.3) | copy-start | bytes 98308
  8.0 205.0 %all-reduce.5.cloned.1.call-start = ((), (), s32[]{:S(2)}) async-start(), calls=%async_computation.2 | async-start | bytes 1769472 | tf_op jit(solution)/shard_map/psum | solution.py:63
  8.1 3.9 %collective-permute-start = (bf16[1,8,64,32]{2,3,1,0:T(8,128)(2,1)}, bf16[1,8,64,32]{2,3,1,0:T(8,128)(2,1)S(1)}, u32[]{:S(2)}, u32[]{:S(2)}) collective-permute-start(bf16[1,8,64,32]{2,3,1,0:T(8,128)(2,1)} %param.3), channel_id=1, source_target_pairs={{0,8},{8,16},{16,24},{24,32},{32,40},{40,48},{48,56},{1,9},{9,17},... | collective-permute-start | bytes 98312 | tf_op jit(solution)/shard_map/ppermute | solution.py:15
  9.8 4.6 %collective-permute-start.1 = (bf16[1,8,64,32]{2,3,1,0:T(8,128)(2,1)}, bf16[1,8,64,32]{2,3,1,0:T(8,128)(2,1)S(1)}, u32[]{:S(2)}, u32[]{:S(2)}) collective-permute-start(bf16[1,8,64,32]{2,3,1,0:T(8,128)(2,1)} %param.3), channel_id=1, source_target_pairs={{8,0},{16,8},{24,16},{32,24},{40,32},{48,40},{56,48},{9,1},{17,9},... | collective-permute-start | bytes 98312 | tf_op jit(solution)/shard_map/ppermute | solution.py:16
  12.0 45.5 %copy-start.8 = (bf16[1,8,64,32]{2,3,1,0:T(8,128)(2,1)}, bf16[1,8,64,32]{2,3,1,0:T(8,128)(2,1)S(1)}, u32[]{:S(2)}) copy-start(bf16[1,8,64,32]{2,3,1,0:T(8,128)(2,1)S(1)} %collective-permute-done) | copy-start | bytes 98308
  14.4 43.9 %copy-start.6 = (bf16[1,8,64,32]{2,3,1,0:T(8,128)(2,1)}, bf16[1,8,64,32]{2,3,1,0:T(8,128)(2,1)S(1)}, u32[]{:S(2)}) copy-start(bf16[1,8,64,32]{2,3,1,0:T(8,128)(2,1)S(1)} %collective-permute-done.1) | copy-start | bytes 98308
  14.5 43.9 %collective-permute-start.3 = (bf16[3,1,64,32]{2,3,1,0:T(8,128)(2,1)S(1)}, bf16[3,1,64,32]{2,3,1,0:T(8,128)(2,1)S(1)}, u32[]{:S(2)}, u32[]{:S(2)}) collective-permute-start(bf16[3,1,64,32]{2,3,1,0:T(8,128)(2,1)S(1)} %get-tuple-element.69), channel_id=1, source_target_pairs={{1,0},{2,1},{3,2},{4,3},{5,4},{6,5},{7,6},{9,8},{10,9},{11,10},{12... | collective-permute-start | bytes 36872 | tf_op jit(solution)/shard_map/ppermute | solution.py:16
  20.5 37.9 %collective-permute-start.2 = (bf16[3,1,64,32]{2,3,1,0:T(8,128)(2,1)S(1)}, bf16[3,1,64,32]{2,3,1,0:T(8,128)(2,1)S(1)}, u32[]{:S(2)}, u32[]{:S(2)}) collective-permute-start(bf16[3,1,64,32]{2,3,1,0:T(8,128)(2,1)S(1)} %get-tuple-element.68), channel_id=1, source_target_pairs={{0,1},{1,2},{2,3},{3,4},{4,5},{5,6},{6,7},{8,9},{9,10},{10,11},{11... | collective-permute-start | bytes 36872 | tf_op jit(solution)/shard_map/ppermute | solution.py:15
  52.3 88.8 %collective-permute-start.5 = (bf16[1,8,64,256]{3,2,1,0:T(8,128)(2,1)S(1)}, bf16[1,8,64,256]{3,2,1,0:T(8,128)(2,1)S(1)}, u32[]{:S(2)}, u32[]{:S(2)}) collective-permute-start(bf16[1,8,64,256]{3,2,1,0:T(8,128)(2,1)S(1)} %copy.99), channel_id=1, source_target_pairs={{8,0},{16,8},{24,16},{32,24},{40,32},{48,40},{56,48},{9,1},{17,9},... | collective-permute-start | bytes 786440 | tf_op jit(solution)/shard_map/ppermute | solution.py:16
  53.6 87.5 %collective-permute-start.4 = (bf16[1,8,64,256]{3,2,1,0:T(8,128)(2,1)S(1)}, bf16[1,8,64,256]{3,2,1,0:T(8,128)(2,1)S(1)}, u32[]{:S(2)}, u32[]{:S(2)}) collective-permute-start(bf16[1,8,64,256]{3,2,1,0:T(8,128)(2,1)S(1)} %copy.99), channel_id=1, source_target_pairs={{0,8},{8,16},{16,24},{24,32},{32,40},{40,48},{48,56},{1,9},{9,17},... | collective-permute-start | bytes 786440 | tf_op jit(solution)/shard_map/ppermute | solution.py:15
  64.3 16.6 %copy-start.15 = (bf16[1,8,64,32]{2,3,1,0:T(8,128)(2,1)S(1)}, bf16[1,8,64,32]{2,3,1,0:T(8,128)(2,1)}, u32[]{:S(2)}) copy-start(bf16[1,8,64,32]{2,3,1,0:T(8,128)(2,1)} %get-tuple-element.52) | copy-start | bytes 98308
  64.3 21.0 %copy-start.14 = (bf16[1,8,64,32]{2,3,1,0:T(8,128)(2,1)S(1)}, bf16[1,8,64,32]{2,3,1,0:T(8,128)(2,1)}, u32[]{:S(2)}) copy-start(bf16[1,8,64,32]{2,3,1,0:T(8,128)(2,1)} %get-tuple-element.51) | copy-start | bytes 98308
  67.2 26.5 %copy-start.13 = (bf16[1,8,64,32]{2,3,1,0:T(8,128)(2,1)S(1)}, bf16[1,8,64,32]{2,3,1,0:T(8,128)(2,1)}, u32[]{:S(2)}) copy-start(bf16[1,8,64,32]{2,3,1,0:T(8,128)(2,1)} %get-tuple-element.48) | copy-start | bytes 98308
  83.8 24.3 %copy-start.12 = (bf16[1,8,64,32]{2,3,1,0:T(8,128)(2,1)S(1)}, bf16[1,8,64,32]{2,3,1,0:T(8,128)(2,1)}, u32[]{:S(2)}) copy-start(bf16[1,8,64,32]{2,3,1,0:T(8,128)(2,1)} %get-tuple-element.44) | copy-start | bytes 98308
  86.0 24.3 %copy-start.3 = (bf16[1,8,64,32]{2,3,1,0:T(8,128)(2,1)S(1)}, bf16[1,8,64,32]{2,3,1,0:T(8,128)(2,1)}, u32[]{:S(2)}) copy-start(bf16[1,8,64,32]{2,3,1,0:T(8,128)(2,1)} %copy-done.2) | copy-start | bytes 98308
  96.7 16.1 %copy-start.9 = (bf16[1,8,64,32]{2,3,1,0:T(8,128)(2,1)S(1)}, bf16[1,8,64,32]{2,3,1,0:T(8,128)(2,1)}, u32[]{:S(2)}) copy-start(bf16[1,8,64,32]{2,3,1,0:T(8,128)(2,1)} %copy-done.8) | copy-start | bytes 98308
  108.7 6.6 %copy-start.1 = (bf16[1,8,64,32]{2,3,1,0:T(8,128)(2,1)S(1)}, bf16[1,8,64,32]{2,3,1,0:T(8,128)(2,1)}, u32[]{:S(2)}) copy-start(bf16[1,8,64,32]{2,3,1,0:T(8,128)(2,1)} %get-tuple-element.60) | copy-start | bytes 98308
  115.3 5.0 %copy-start.5 = (bf16[1,8,64,32]{2,3,1,0:T(8,128)(2,1)S(1)}, bf16[1,8,64,32]{2,3,1,0:T(8,128)(2,1)}, u32[]{:S(2)}) copy-start(bf16[1,8,64,32]{2,3,1,0:T(8,128)(2,1)} %param.3) | copy-start | bytes 98308
  122.8 5.0 %copy-start.7 = (bf16[1,8,64,32]{2,3,1,0:T(8,128)(2,1)S(1)}, bf16[1,8,64,32]{2,3,1,0:T(8,128)(2,1)}, u32[]{:S(2)}) copy-start(bf16[1,8,64,32]{2,3,1,0:T(8,128)(2,1)} %copy-done.6) | copy-start | bytes 98308
  128.7 3.5 %copy-start.18 = (bf16[512,32]{0,1:T(8,128)(2,1)S(1)}, bf16[512,32]{0,1:T(8,128)(2,1)}, u32[]{:S(2)}) copy-start(bf16[512,32]{0,1:T(8,128)(2,1)} %reshape.324) | copy-start | bytes 98308
  132.1 82.1 %reduce-scatter.2.cloned.1.call-start = ((), (), s32[]{:S(2)}) async-start(), calls=%async_computation.1 | async-start | bytes 1179648 | tf_op jit(solution)/shard_map/reduce_scatter | solution.py:36
  141.2 7.7 %collective-permute-start.7 = (bf16[3,1,64,256]{3,2,1,0:T(8,128)(2,1)S(1)}, bf16[3,1,64,256]{3,2,1,0:T(8,128)(2,1)S(1)}, u32[]{:S(2)}, u32[]{:S(2)}) collective-permute-start(bf16[3,1,64,256]{3,2,1,0:T(8,128)(2,1)S(1)} %get-tuple-element.40), channel_id=1, source_target_pairs={{1,0},{2,1},{3,2},{4,3},{5,4},{6,5},{7,6},{9,8},{10,9},{11,10},{12... | collective-permute-start | bytes 294920 | tf_op jit(solution)/shard_map/ppermute | solution.py:16
  143.5 6.5 %collective-permute-start.6 = (bf16[3,1,64,256]{3,2,1,0:T(8,128)(2,1)S(1)}, bf16[3,1,64,256]{3,2,1,0:T(8,128)(2,1)S(1)}, u32[]{:S(2)}, u32[]{:S(2)}) collective-permute-start(bf16[3,1,64,256]{3,2,1,0:T(8,128)(2,1)S(1)} %get-tuple-element.39), channel_id=1, source_target_pairs={{0,1},{1,2},{2,3},{3,4},{4,5},{5,6},{6,7},{8,9},{9,10},{10,11},{11... | collective-permute-start | bytes 294920 | tf_op jit(solution)/shard_map/ppermute | solution.py:15
  148.6 138.5 %all-reduce.7.cloned.1.call-start = ((), (), s32[]{:S(2)}) async-start(), calls=%async_computation.3 | async-start | bytes 1769472 | tf_op jit(solution)/shard_map/psum | solution.py:63
  (25 other events, 20.8 us)
Sparse Core Ops, SparseCore 0:
  132.2 80.7 all-reduce.4
  215.5 71.5 all-reduce.6
Sparse Core Ops, SparseCore 1:
  148.7 42.0 reduce-scatter.1
